TPU v7x, 512 devices: a whole 4x8x8 slice. The times are simulated.
512 devices in a mesh: inp: 128 (over y, z, core), vis: 4 (over x).
Axes of the slice: x: 4, y: 8, z: 8, core: 2. Of those that a mesh axis runs over, the one named last changes fastest.
Arguments:
- samples: bfloat16 [128, 2048, 2048], P('vis', 'inp'), may hold values from -6 to 6
- history: bfloat16 [3, 2048, 2048], P(None, 'inp'), may hold values from -6 to 6
- fir_taps: float32 [4, 2048], replicated, may hold values from -3 to 3
- kept_channels: int32 [128], replicated, may hold values from 0 to 1023, as said below
Outputs:
- visibility: bfloat16 [128, 2048, 2048], P('inp', 'vis')
Inputs may be any that keep to these rules, and one draw needn't show every extreme that they name: `kept_channels`: 128 distinct channel numbers in no particular order; channels 0 and 1023 are always among them.
All inputs are finite; a program needn't handle non-finite values.
Results may differ from a plain program's by a relative error of at most 0.0078.
Values may be sent and summed in bfloat16 or wider, within the bound.
A program may use at most 64 MiB of HBM per device.

v0:
```python
from functools import partial
import math

import jax
import jax.numpy as jnp
from jax import lax
from jax.sharding import PartitionSpec as P

TAPS = 4
CH_DEV = 1


def shifted(value, axis, steps):
    count = lax.axis_size(axis)
    initial, last = (max(0, -steps), min(count, count - steps))
    return lax.ppermute(value, axis, [(source, source + steps) for source in range(initial, last)])


def make_table(kept_channels, sample_count):
    positions = jnp.arange(sample_count, dtype=jnp.int32)
    products = kept_channels[:, None] * positions[None, :] % sample_count
    angles = products.astype(jnp.float32) * (2.0 * math.pi / sample_count)
    norm_scale = 1.0 / math.sqrt(sample_count)
    table = jnp.concatenate([jnp.cos(angles) * norm_scale, -jnp.sin(angles) * norm_scale], axis=0)
    return table.astype(jnp.bfloat16)


def add_frames(running, shard_piece, offset, vis_index, row_count):
    real_part = shard_piece[0]
    imag_part = shard_piece[1]
    stacked = jnp.concatenate([real_part, imag_part], axis=1)
    rotated = jnp.concatenate([-imag_part, real_part], axis=1)
    row_block = lax.dynamic_slice_in_dim(stacked, vis_index * row_count, row_count, 2)
    input_total = stacked.shape[2]
    re_block = jnp.einsum("cfa,cfb->cab", row_block, stacked, preferred_element_type=jnp.float32)
    im_block = jnp.einsum("cfa,cfb->cab", row_block, rotated, preferred_element_type=jnp.float32)
    row_ids = vis_index * row_count + jnp.arange(row_count, dtype=jnp.int32)
    col_ids = jnp.arange(input_total, dtype=jnp.int32)
    contribution = jnp.where(col_ids[None, None, :] >= row_ids[None, :, None], re_block, im_block)
    return contribution


def per_device(samples, history, fir_taps, kept_channels):
    vis_count = lax.axis_size("vis")
    vis_index = lax.axis_index("vis")
    inp_count = lax.axis_size("inp")
    frame_count, input_count, sample_count = samples.shape
    history_len = TAPS - 1
    previous = shifted(samples[frame_count - history_len :], "vis", 1)
    previous = jnp.where(vis_index == 0, history, previous)
    extended = jnp.concatenate([previous, samples], axis=0)
    weighted = fir_taps[0][None, None, :] * extended[0:frame_count].astype(jnp.float32)
    for tap_index in range(1, TAPS):
        weighted = weighted + fir_taps[tap_index][None, None, :] * extended[
            tap_index : tap_index + frame_count
        ].astype(jnp.float32)
    weighted = weighted.astype(jnp.bfloat16)
    dft_table = make_table(kept_channels, sample_count)
    kept_total = kept_channels.shape[0]
    spectra = jnp.einsum(
        "kn,fin->kfi", dft_table, weighted, preferred_element_type=jnp.float32
    ).astype(jnp.bfloat16)
    spectra = spectra.reshape(2, kept_total, frame_count, input_count)
    input_total = input_count * inp_count
    row_count = input_total // vis_count
    frame_total = frame_count * vis_count
    initial = jnp.zeros((CH_DEV, row_count, input_total), jnp.float32)
    correlate = partial(add_frames, vis_index=vis_index, row_count=row_count)
    all_frames = lax.all_gather(spectra, "vis", axis=2, tiled=True)
    channel_data = lax.all_to_all(all_frames, "inp", split_axis=1, concat_axis=3, tiled=True)
    summed = correlate(initial, channel_data, 0)
    return (summed / float(frame_total)).astype(jnp.bfloat16)


def solution(mesh):
    return jax.shard_map(
        per_device,
        mesh=mesh,
        in_specs=(P("vis", "inp", None), P(None, "inp", None), P(), P()),
        out_specs=P("inp", "vis", None),
        check_vma=False,
    )
```

profile of v0, /device:TPU:1, one launch (start us, length us, event | category | flops | bytes accessed | tf_op | source)
XLA Modules:
  0.0 116.5 jit_solution(1827298505399509753)
XLA Ops:
  6.5 0.0 copy-start
  6.5 0.0 all-gather.2.cloned.1.call-start
  6.5 1.1 slice.33
  7.6 4.0 %collective-permute-start = (bf16[3,16,2048]{2,1,0:T(8,128)(2,1)S(1)}, bf16[3,16,2048]{2,1,0:T(8,128)(2,1)S(1)}, u32[]{:S(2)}, u32[]{:S(2)}) collective-permute-start(bf16[3,16,2048]{2,1,0:T(8,128)(2,1)S(1)} %slice.33), channel_id=1, source_target_pairs={{0,1},{1,2},{2,3},{4,5},{5,6},{6,7},{8,9},{9,10},{10,11},{12,13},{... | collective-permute-start | bytes 589832 | tf_op jit(solution)/shard_map/ppermute | solution.py:16
  11.6 5.6 %multiply_convert_fusion.2 = (bf16[128,2048]{1,0:T(8,128)(2,1)S(1)}, bf16[128,2048]{1,0:T(8,128)(2,1)S(1)}) fusion(s32[128]{0:T(128)} %param.7), kind=kLoop, calls=%fused_computation.33 | loop fusion | flops 4980736 | bytes 1049088 | tf_op jit(solution)/shard_map/convert
  17.2 1.5 %fusion.29 = (f32[1,2048]{1,0:T(1,128)S(1)}, f32[1,2048]{1,0:T(1,128)S(1)}, f32[1,2048]{1,0:T(1,128)}, f32[1,2048]{1,0:T(1,128)}) fusion(f32[4,2048]{1,0:T(4,128)} %param.6), kind=kLoop, calls=%fused_computation.46 | loop fusion | bytes 65536 | tf_op jit(solution)/shard_map/slice | solution.py:52
  18.8 0.0 collective-permute-done
  18.8 1.0 broadcast_select_fusion
  19.7 0.0 copy-done
  19.7 2.7 %add_convert_fusion = bf16[32,16,2048]{2,1,0:T(8,128)(2,1)S(1)} fusion(bf16[32,16,2048]{2,1,0:T(8,128)(2,1)S(1)} %copy-done, bf16[3,16,2048]{2,1,0:T(8,128)(2,1)S(1)} %broadcast_select_fusion, f32[2048]{0:T(1024)} %bitcast.36, f32[2048]{0:T(1024)} %bitcast.37, f32[2048]{0:T(1024)S(1)} %bitcast.35, f32[2048]{0:T(1024)S(1)} %bitcast.34), kind=kLoop, calls=%fused_computation.1 | loop fusion | flops 15728640 | bytes 4423680 | tf_op jit(solution)/shard_map/convert_element_type | solution.py:57
  22.5 1.6 %fusion.5 = bf16[256,32,16]{0,1,2:T(8,128)(2,1)S(1)} fusion(bf16[32,16,2048]{2,1,0:T(8,128)(2,1)S(1)} %add_convert_fusion, bf16[128,2048]{1,0:T(8,128)(2,1)S(1)} %get-tuple-element.12, bf16[128,2048]{1,0:T(8,128)(2,1)S(1)} %get-tuple-element.11), kind=kOutput, calls=%fused_computation.16 | convolution fusion | flops 539099136 | bytes 3407872 | tf_op jit(solution)/shard_map/kn,fin->kfi/dot_general | solution.py:60
  24.1 0.1 reshape.47
  24.2 1.0 copy.9
  25.2 0.0 all-gather.2.cloned.1.call-update
  25.2 32.2 %all-gather.2.cloned.1.call-done = bf16[2,128,128,16]{1,3,0,2:T(8,128)(2,1)} async-done(((bf16[2,128,32,16]{1,3,0,2:T(8,128)(2,1)}), bf16[2,128,128,16]{1,3,0,2:T(8,128)(2,1)}) %all-gather.2.cloned.1.call-update) | async-done | bytes 1048592 | tf_op jit(solution)/shard_map/all_gather | solution.py:69
  57.5 3.2 %copy.10 = bf16[2,128,128,16]{2,3,0,1:T(8,128)(2,1)} copy(bf16[2,128,128,16]{1,3,0,2:T(8,128)(2,1)} %all-gather.2.cloned.1.call-done) | data formatting | bytes 2097152 | tf_op jit(solution)/shard_map/all_gather | solution.py:69
  60.7 15.2 %all-to-all-start = ((bf16[2,128,128,16]{2,3,0,1:T(8,128)(2,1)}), bf16[2,128,128,16]{2,3,0,1:T(8,128)(2,1)S(1)}, u32[]{:S(2)}, u32[]{:S(2)}) async-start(bf16[2,128,128,16]{2,3,0,1:T(8,128)(2,1)} %copy.10), calls=%async_computation | async-start | bytes 2097152 | tf_op jit(solution)/shard_map/all_to_all | solution.py:70
  75.9 30.4 %all-to-all-done = bf16[2,128,128,16]{2,3,0,1:T(8,128)(2,1)S(1)} async-done(((bf16[2,128,128,16]{2,3,0,1:T(8,128)(2,1)}), bf16[2,128,128,16]{2,3,0,1:T(8,128)(2,1)S(1)}, u32[]{:S(2)}, u32[]{:S(2)}) %all-to-all-start) | async-done | bytes 1048608 | tf_op jit(solution)/shard_map/all_to_all | solution.py:70
  106.3 0.2 copy.17
  106.5 0.2 fusion.28
  106.7 0.1 bitcast_negate_fusion
  106.8 0.7 fusion.9
  107.5 2.1 %fusion = bf16[1,512,2048]{2,1,0:T(8,128)(2,1)} fusion(f32[512,2048]{1,0:T(8,128)S(1)} %fusion.9, s32[512]{0:T(512)S(1)} %iota_add_fusion, bf16[1,128,2048]{1,2,0:T(8,128)(2,1)S(1)} %bitcast.30, bf16[1,128,2048]{1,2,0:T(8,128)(2,1)S(1)} %bitcast_negate_fusion, s32[]{:T(128)S(6)} %select_n.26, bf16[1,128,2048]{1,2,0:T(8,128)(2,1)S(1)} %bitcast.32), kind=kOutput, calls=%fused_computation.5 | convolution fusion | flops 543686656 | bytes 8390660 | tf_op jit(solution)/shard_map/cfa,cfb->cab/dot_general | solution.py:36
  (1 shorter events, 0.0 us)
Async XLA Ops:
  6.5 13.2 %copy-start = (bf16[32,16,2048]{2,1,0:T(8,128)(2,1)S(1)}, bf16[32,16,2048]{2,1,0:T(8,128)(2,1)}, u32[]{:S(2)}) copy-start(bf16[32,16,2048]{2,1,0:T(8,128)(2,1)} %param.4) | copy-start | bytes 6291460
  6.5 50.9 %all-gather.2.cloned.1.call-start = ((), (), s32[]{:S(2)}) async-start(), calls=%async_computation.1 | async-start | bytes 1310720 | tf_op jit(solution)/shard_map/all_gather | solution.py:69
  7.6 11.1 %collective-permute-start = (bf16[3,16,2048]{2,1,0:T(8,128)(2,1)S(1)}, bf16[3,16,2048]{2,1,0:T(8,128)(2,1)S(1)}, u32[]{:S(2)}, u32[]{:S(2)}) collective-permute-start(bf16[3,16,2048]{2,1,0:T(8,128)(2,1)S(1)} %slice.33), channel_id=1, source_target_pairs={{0,1},{1,2},{2,3},{4,5},{5,6},{6,7},{8,9},{9,10},{10,11},{12,13},{... | collective-permute-start | bytes 589832 | tf_op jit(solution)/shard_map/ppermute | solution.py:16
  60.7 45.6 %all-to-all-start = ((bf16[2,128,128,16]{2,3,0,1:T(8,128)(2,1)}), bf16[2,128,128,16]{2,3,0,1:T(8,128)(2,1)S(1)}, u32[]{:S(2)}, u32[]{:S(2)}) async-start(bf16[2,128,128,16]{2,3,0,1:T(8,128)(2,1)} %copy.10), calls=%async_computation | async-start | bytes 2097152 | tf_op jit(solution)/shard_map/all_to_all | solution.py:70
Sparse Core Ops, SparseCore 0:
  25.4 32.0 all-gather.1
where the time goes:
time: 117 us
  waiting for transfers between devices  62.7 us (54%)
  starting transfers between devices  19.2 us (16%)
  between operations  13.5 us (12%)
  other arithmetic  9.41 us (8%)
  local copies, waits for them, and re-layouts  7.24 us (6%)
  matrix products  4.52 us (4%)
    all_gather x1, waiting for transfers between devices, per_device(): all_frames = lax.all_gather(spectra, 'vis', axis=2, tiled=True)  32.2 us
    all_to_all x1, waiting for transfers between devices, per_device(): lax.all_to_all(all_frames, 'inp', split_axis=1, concat_axis=3, tiled=True)  30.4 us
    all_to_all x1, starting transfers between devices, per_device(): lax.all_to_all(all_frames, 'inp', split_axis=1, concat_axis=3, tiled=True)  15.2 us
    another operation x1, other arithmetic  5.62 us
    ppermute x1, starting transfers between devices, shifted(): lax.ppermute(value, axis, [(source, source + steps) for source in range(i...  3.96 us
    all_gather x1, local copies, waits for them, and re-layouts, per_device(): all_frames = lax.all_gather(spectra, 'vis', axis=2, tiled=True)  3.17 us
    convert_element_type x1, other arithmetic, per_device(): weighted = weighted.astype(jnp.bfloat16)  2.74 us
  transfers between devices with their start and end apart: 3, of which 2 were waited for; matrix products, arithmetic and copies ran while one was open for 6% of the time, Pallas kernels for 0%

commit v1 on v0

v1 whole, which is shorter than its diff:
```python
import functools
import math

import jax
import jax.numpy as jnp
from jax import lax
from jax.experimental import pallas as pl
from jax.experimental.pallas import tpu as pltpu
from jax.sharding import PartitionSpec as P

TAPS = 4
MESH = pl.DeviceIdType.MESH
NI, NV, NY, NZ = 128, 4, 8, 8
ZGROUPS = ((0,), (1, 7), (2, 6), (3, 5), (4,))
DEPTH = 1


def exchange_kernel(z_ref, g_ref, a_send, a_recv, l_sem, x_send, x_recv):
    me = lax.axis_index("inp")
    v = lax.axis_index("vis")
    y, z, c = me // 16, lax.rem(me // 2, 8), lax.rem(me, 2)
    right, left, opp = lax.rem(v + 1, NV), lax.rem(v + 3, NV), lax.rem(v + 2, NV)

    barrier = pltpu.get_barrier_semaphore()

    def greet(d, _):
        pl.semaphore_signal(barrier, inc=1, device_id=(lax.rem(me + d, NI), v), device_id_type=MESH)
        return 0

    lax.fori_loop(1, NI, greet, 0)
    for other in (left, right):
        pl.semaphore_signal(barrier, inc=1, device_id=(me, other), device_id_type=MESH)
    pl.semaphore_wait(barrier, NI - 1 + 2)

    own = pltpu.make_async_copy(z_ref.at[me], g_ref.at[v, y, z, c], l_sem)
    own.start()

    def send(dy, dz, dc):
        ty, tz, tc = lax.rem(y + dy, 8), lax.rem(z + dz, 8), lax.rem(c + dc, 2)
        pltpu.make_async_remote_copy(
            src_ref=z_ref.at[ty * 16 + tz * 2 + tc],
            dst_ref=g_ref.at[v, y, z, c],
            send_sem=a_send,
            recv_sem=a_recv.at[(8 - dz) % 8],
            device_id=(ty * 16 + tz * 2 + tc, v),
            device_id_type=MESH,
        ).start()

    for group in ZGROUPS:
        if group == (0,):
            send(0, 0, 1)

        def body(dy, _, group=group):
            for dc in (0, 1):
                for dz in group:
                    send(dy, dz, dc)
            return 0

        lax.fori_loop(1 if group == (0,) else 0, 8, body, 0)
    own.wait()

    def whole(vv, tz):
        return g_ref.at[vv, :, tz]

    def half(vv, tz, h):
        return g_ref.at[vv, pl.ds(4 * h, 4), tz]

    def relay(k):
        for dz in ZGROUPS[k]:
            tz = lax.rem(z + dz, 8)
            for side, (source, target) in enumerate(((left, right), (right, left))):
                pltpu.make_async_copy(whole(source, tz), whole(source, tz), x_recv.at[dz, side]).wait()
                pltpu.make_async_remote_copy(
                    src_ref=half(source, tz, side),
                    dst_ref=half(source, tz, side),
                    send_sem=x_send.at[2],
                    recv_sem=x_recv.at[dz, 2 + side],
                    device_id=(me, target),
                    device_id_type=MESH,
                ).start()

    for k, group in enumerate(ZGROUPS):
        for dz in group:
            tz = lax.rem(z + dz, 8)
            if dz == 0:
                pltpu.make_async_copy(z_ref.at[pl.ds(0, 15)], z_ref.at[pl.ds(0, 15)], a_recv.at[0]).wait()
            else:
                pltpu.make_async_copy(whole(v, tz), whole(v, tz), a_recv.at[dz]).wait()
            for side, target in enumerate((right, left)):
                pltpu.make_async_remote_copy(
                    src_ref=whole(v, tz),
                    dst_ref=whole(v, tz),
                    send_sem=x_send.at[side],
                    recv_sem=x_recv.at[dz, side],
                    device_id=(me, target),
                    device_id_type=MESH,
                ).start()
        if k >= DEPTH:
            relay(k - DEPTH)
    for k in range(len(ZGROUPS) - DEPTH, len(ZGROUPS)):
        relay(k)
    for dz in range(8):
        tz = lax.rem(z + dz, 8)
        for side in range(2):
            pltpu.make_async_copy(half(opp, tz, side), half(opp, tz, side), x_recv.at[dz, 2 + side]).wait()
    for i in range(3):
        pltpu.make_async_copy(g_ref.at[v], g_ref.at[v], x_send.at[i]).wait()
    pltpu.make_async_copy(z_ref.at[pl.ds(0, NI - 1)], z_ref.at[pl.ds(0, NI - 1)], a_send).wait()


def exchange(blocks):
    return pl.pallas_call(
        exchange_kernel,
        out_shape=jax.ShapeDtypeStruct((NV, NY, NZ, 2, 8, 128), jnp.bfloat16),
        in_specs=[pl.BlockSpec(memory_space=pltpu.VMEM)],
        out_specs=pl.BlockSpec(memory_space=pltpu.VMEM),
        scratch_shapes=[
            pltpu.SemaphoreType.DMA,
            pltpu.SemaphoreType.DMA((8,)),
            pltpu.SemaphoreType.DMA,
            pltpu.SemaphoreType.DMA((3,)),
            pltpu.SemaphoreType.DMA((8, 4)),
        ],
        compiler_params=pltpu.CompilerParams(collective_id=0, has_side_effects=True),
    )(blocks)


def make_table(kept_channels, sample_count):
    low = jnp.arange(128, dtype=jnp.int32)
    high = jnp.arange(sample_count // 128, dtype=jnp.int32) * 128
    step = 2.0 * math.pi / sample_count

    def pair(n):
        angle = (kept_channels[:, None] * n[None, :] % sample_count).astype(jnp.float32) * step
        return jnp.cos(angle), jnp.sin(angle)

    (cl, sl), (ch, sh) = pair(low), pair(high)
    scale = 1.0 / math.sqrt(sample_count)
    cl, sl = (cl * scale)[:, None, :], (sl * scale)[:, None, :]
    ch, sh = ch[:, :, None], sh[:, :, None]
    real = ch * cl - sh * sl
    imag = -(sh * cl + ch * sl)
    count = kept_channels.shape[0]
    return jnp.concatenate([real, imag], axis=0).reshape(2 * count, sample_count).astype(jnp.bfloat16)


def shifted(value, axis, steps):
    count = lax.axis_size(axis)
    initial, last = (max(0, -steps), min(count, count - steps))
    return lax.ppermute(value, axis, [(source, source + steps) for source in range(initial, last)])


def per_device(samples, history, fir_taps, kept_channels):
    vis_index = lax.axis_index("vis")
    frame_count, input_count, sample_count = samples.shape
    previous = shifted(samples[frame_count - TAPS + 1 :], "vis", 1)
    previous = jnp.where(vis_index == 0, history, previous)
    extended = jnp.concatenate([previous, samples], axis=0)
    weighted = fir_taps[0][None, None, :] * extended[0:frame_count].astype(jnp.float32)
    for tap_index in range(1, TAPS):
        weighted = weighted + fir_taps[tap_index][None, None, :] * extended[
            tap_index : tap_index + frame_count
        ].astype(jnp.float32)
    weighted = weighted.astype(jnp.bfloat16)
    table = make_table(kept_channels, sample_count)
    spectra = jnp.einsum("kn,fin->kfi", table, weighted, preferred_element_type=jnp.float32)
    spectra = spectra.astype(jnp.bfloat16).reshape(2, NI, frame_count, 2, 8)
    blocks = spectra.transpose(1, 4, 0, 3, 2).reshape(NI, 8, 128)
    gathered = exchange(blocks)

    gathered = gathered.reshape(NV, NI, 8, 2, 2, frame_count)
    parts = gathered.transpose(3, 1, 4, 2, 0, 5).reshape(2, NI * input_count, NV * frame_count)
    real, imag = parts[0], parts[1]
    rows = NI * input_count // NV
    both = jnp.concatenate([real, imag], axis=1)
    turned = jnp.concatenate([-imag, real], axis=1)
    block = lax.dynamic_slice_in_dim(both, vis_index * rows, rows, 0)
    dims = (((1,), (1,)), ((), ()))
    re_block = lax.dot_general(block, both, dims, preferred_element_type=jnp.float32)
    im_block = lax.dot_general(block, turned, dims, preferred_element_type=jnp.float32)
    row_ids = vis_index * rows + jnp.arange(rows, dtype=jnp.int32)
    col_ids = jnp.arange(NI * input_count, dtype=jnp.int32)
    out = jnp.where(col_ids[None, :] >= row_ids[:, None], re_block, im_block)
    return (out / float(NV * frame_count)).astype(jnp.bfloat16)[None]


def solution(mesh):
    return jax.shard_map(
        per_device,
        mesh=mesh,
        in_specs=(P("vis", "inp", None), P(None, "inp", None), P(), P()),
        out_specs=P("inp", "vis", None),
        check_vma=False,
    )
```

time: 117 us -> 85.5 us (0.73)
  waiting for transfers between devices: 62.7 us -> 0.01 us
  Pallas kernels: 0 us -> 37.7 us
  local copies, waits for them, and re-layouts: 7.24 us -> 28.6 us
  starting transfers between devices: 19.2 us -> 4.63 us
  between operations: 13.5 us -> 0.14 us
  other arithmetic: 9.41 us -> 6.81 us
  matrix products: 4.52 us -> 6.84 us
    pallas_call x0 -> x1, Pallas kernels: none -> 37.7 us  [exchange(): pl.pallas_call(exchange_kernel, out_shape=jax.ShapeDtypeStruct((NV, NY, N...]
    all_gather x1 -> x0, waiting for transfers between devices: 32.2 us -> none  [per_device(): all_frames = lax.all_gather(spectra, 'vis', axis=2, tiled=True)]
    all_to_all x1 -> x0, waiting for transfers between devices: 30.4 us -> none  [per_device(): lax.all_to_all(all_frames, 'inp', split_axis=1, concat_axis=3, tiled=True)]
    all_to_all x1 -> x0, starting transfers between devices: 15.2 us -> none  [per_device(): lax.all_to_all(all_frames, 'inp', split_axis=1, concat_axis=3, tiled=True)]
    slice x2 -> x4, local copies, waits for them, and re-layouts: 1.27 us -> 13.6 us  [the longest x3 12.6 us: per_device(): real, imag = (parts[0], parts[1])]
    reshape x2 -> x4, local copies, waits for them, and re-layouts: 1.08 us -> 10.7 us  [the longest x1 9.74 us: per_device(): gathered = gathered.reshape(NV, NI, 8, 2, 2, frame_count)]
    another operation x1, other arithmetic: 5.62 us -> 0.71 us
    all_gather x1 -> x0, local copies, waits for them, and re-layouts: 3.17 us -> none  [per_device(): all_frames = lax.all_gather(spectra, 'vis', axis=2, tiled=True)]
  transfers between devices with their start and end apart: 3 -> 1, of which waited for: 2 -> 0; matrix products, arithmetic and copies ran while one was open for 6% -> 5% of each run, Pallas kernels for 0% -> 0%
where the time goes in v1:
time: 85.5 us; the launch traced here: 84.7 us
  Pallas kernels  37.7 us (44%)
  local copies, waits for them, and re-layouts  28.6 us (33%)
  matrix products  6.84 us (8%)
  other arithmetic  6.81 us (8%)
  starting transfers between devices  4.63 us (5%)
    pallas_call x1, Pallas kernels, exchange(): pl.pallas_call(exchange_kernel, out_shape=jax.ShapeDtypeStruct((NV, NY, N...  37.7 us
    slice x3, local copies, waits for them, and re-layouts, per_device(): real, imag = (parts[0], parts[1])  12.6 us
    reshape x1, local copies, waits for them, and re-layouts, per_device(): gathered = gathered.reshape(NV, NI, 8, 2, 2, frame_count)  9.74 us
    ppermute x1, starting transfers between devices, shifted(): lax.ppermute(value, axis, [(source, source + steps) for source in range(i...  4.63 us
    dot_general x1, matrix products, per_device(): lax.dot_general(block, turned, dims, preferred_element_type=jnp.float32)  3.14 us
    convert_element_type x1, other arithmetic, per_device(): weighted = weighted.astype(jnp.bfloat16)  2.74 us
    squeeze x2, local copies, waits for them, and re-layouts, per_device(): real, imag = (parts[0], parts[1])  2.29 us
    dot_general x1, matrix products, per_device(): lax.dot_general(block, both, dims, preferred_element_type=jnp.float32)  2.06 us
  transfers between devices with their start and end apart: 1, of which 0 were waited for; matrix products, arithmetic and copies ran while one was open for 5% of the time, Pallas kernels for 0%

profile of v1, /device:TPU:1, one launch (start us, length us, event | category | flops | bytes accessed | tf_op | source)
XLA Modules:
  0.0 84.7 jit_solution(687582079294331647)
XLA Ops:
  0.0 0.0 copy-start.1
  0.0 1.0 %slice.33 = bf16[3,16,2048]{2,1,0:T(8,128)(2,1)S(1)} slice(bf16[32,16,2048]{2,1,0:T(8,128)(2,1)} %param.4), slice={[29:32], [0:16], [0:2048]} | slice | bytes 393216 | tf_op jit(solution)/shard_map/slice | solution.py:156
  1.0 4.6 %collective-permute-start = (bf16[3,16,2048]{2,1,0:T(8,128)(2,1)S(1)}, bf16[3,16,2048]{2,1,0:T(8,128)(2,1)}, u32[]{:S(2)}, u32[]{:S(2)}) collective-permute-start(bf16[3,16,2048]{2,1,0:T(8,128)(2,1)S(1)} %slice.33), channel_id=1, source_target_pairs={{0,1},{1,2},{2,3},{4,5},{5,6},{6,7},{8,9},{9,10},{10,11},{12,13},{... | collective-permute-start | bytes 589832 | tf_op jit(solution)/shard_map/ppermute | solution.py:150
  5.6 1.0 %cosine_multiply_fusion = (f32[128,128]{1,0:T(8,128)S(1)}, f32[128,128]{1,0:T(8,128)S(1)}) fusion(s32[128]{0:T(128)} %param.7), kind=kLoop, calls=%fused_computation.35 | loop fusion | flops 262144 | bytes 131584 | tf_op jit(solution)/shard_map/mul | solution.py:139
  6.6 0.8 fusion.26
  7.4 0.1 copy.12
  7.5 0.0 copy-start
  7.5 0.1 copy.13
  7.6 0.0 copy-start.2
  7.6 0.7 subtract_convert_fusion
  8.3 0.2 copy_bitcast_fusion
  8.6 0.0 copy-done.2
  8.6 0.6 fusion.33
  9.2 0.6 iota_add_fusion
  9.8 0.0 collective-permute-done
  9.8 0.0 copy-done.1
  9.8 0.0 copy-done
  9.8 2.7 %add_convert_fusion = bf16[32,16,2048]{2,1,0:T(8,128)(2,1)S(1)} fusion(bf16[32,16,2048]{2,1,0:T(8,128)(2,1)S(1)} %copy-done, bf16[3,16,2048]{2,1,0:T(8,128)(2,1)S(1)} %broadcast_select_fusion, f32[2048]{0:T(1024)} %bitcast.30, f32[2048]{0:T(1024)} %bitcast.31, f32[2048]{0:T(1024)S(1)} %bitcast.29, f32[2048]{0:T(1024)S(1)} %bitcast.28), kind=kLoop, calls=%fused_computation.1 | loop fusion | flops 15728640 | bytes 4423680 | tf_op jit(solution)/shard_map/convert_element_type | solution.py:164
  12.6 1.6 %fusion.5 = bf16[256,32,16]{0,1,2:T(8,128)(2,1)S(1)} fusion(bf16[32,16,2048]{2,1,0:T(8,128)(2,1)S(1)} %add_convert_fusion, bf16[128,2048]{1,0:T(8,128)(2,1)S(1)} %get-tuple-element.19, bf16[128,2048]{1,0:T(8,128)(2,1)S(1)} %get-tuple-element.20), kind=kOutput, calls=%fused_computation.13 | convolution fusion | flops 539099136 | bytes 3407872 | tf_op jit(solution)/shard_map/kn,fin->kfi/dot_general | solution.py:166
  14.2 0.1 reshape.159
  14.4 0.9 %copy.16.z_ref = bf16[128,8,128]{2,1,0:T(8,128)(2,1)} copy(bf16[128,8,128]{0,2,1:T(8,128)(2,1)S(1)} %bitcast.27) | data formatting | bytes 524288 | tf_op jit(solution)/shard_map/reshape | solution.py:168
  15.3 37.7 %shard_map.46 = bf16[4,8,8,2,8,128]{5,4,3,2,1,0:T(8,128)(2,1)} custom-call(bf16[128,8,128]{2,1,0:T(8,128)(2,1)} %copy.16.z_ref), custom_call_target="tpu_custom_call" | custom-call | tf_op jit(solution)/shard_map/pallas_call | solution.py:112
  53.0 9.7 %reshape.161 = bf16[4,128,8,2,2,32]{5,4,3,2,1,0:T(2,128)(2,1)} reshape(bf16[4,8,8,2,8,128]{5,4,3,2,1,0:T(8,128)(2,1)} %shard_map.46) | data formatting | bytes 2097152 | tf_op jit(solution)/shard_map/reshape | solution.py:171
  62.7 5.7 %fusion.31 = (bf16[1,128,2,8,4,32]{5,2,0,3,1,4:T(2,128)(2,1)}, bf16[1,128,2,8,4,32]{5,2,0,3,1,4:T(2,128)(2,1)S(1)}) fusion(bf16[2,128,2,8,4,32]{5,2,0,3,1,4:T(2,128)(2,1)} %bitcast.24), kind=kLoop, calls=%fused_computation.57 | loop fusion | bytes 2097152 | tf_op jit(solution)/shard_map/slice | solution.py:173
  68.4 2.7 %copy.17 = bf16[1,128,2,8,4,32]{5,4,3,2,1,0:T(4,128)(2,1)S(1)} copy(bf16[1,128,2,8,4,32]{5,2,0,3,1,4:T(2,128)(2,1)S(1)} %get-tuple-element.6) | data formatting | bytes 1048576 | tf_op jit(solution)/shard_map/slice | solution.py:173
  71.1 1.2 %squeeze.6 = bf16[2048,128]{1,0:T(8,128)(2,1)S(1)} reshape(bf16[1,128,2,8,4,32]{5,4,3,2,1,0:T(4,128)(2,1)S(1)} %copy.17) | data formatting | bytes 1048576 | tf_op jit(solution)/shard_map/squeeze | solution.py:173
  72.3 0.9 %constant_dynamic-update-slice_fusion.1 = bf16[2048,256]{1,0:T(8,128)(2,1)} fusion(bf16[2048,128]{1,0:T(8,128)(2,1)S(1)} %squeeze.6), kind=kLoop, calls=%fused_computation.48 | loop fusion | bytes 1048576
  73.2 4.3 %copy.18 = bf16[1,128,2,8,4,32]{5,4,3,2,1,0:T(4,128)(2,1)S(1)} copy(bf16[1,128,2,8,4,32]{5,2,0,3,1,4:T(2,128)(2,1)} %get-tuple-element.5) | data formatting | bytes 1048576 | tf_op jit(solution)/shard_map/slice | solution.py:173
  77.5 1.1 %squeeze.7 = bf16[2048,128]{1,0:T(8,128)(2,1)S(1)} reshape(bf16[1,128,2,8,4,32]{5,4,3,2,1,0:T(4,128)(2,1)S(1)} %copy.18) | data formatting | bytes 1048576 | tf_op jit(solution)/shard_map/squeeze | solution.py:173
  78.5 1.0 %fusion.32 = (bf16[2048,128]{1,0:T(8,128)(2,1)S(1)}, bf16[2048,256]{1,0:T(8,128)(2,1)}) fusion(bf16[2048,128]{1,0:T(8,128)(2,1)S(1)} %squeeze.7, bf16[2048,256]{1,0:T(8,128)(2,1)} %constant_dynamic-update-slice_fusion.1), kind=kLoop, calls=%fused_computation.58 | loop fusion | flops 786432 | bytes 1572864 | tf_op jit(solution)/shard_map/neg | solution.py:176
  79.5 0.0 copy-start.3
  79.5 2.1 %fusion.14 = f32[512,2048]{1,0:T(8,128)S(1)} fusion(bf16[2048,256]{1,0:T(8,128)(2,1)} %get-tuple-element.8, s32[]{:T(128)S(6)} %select_n.46), kind=kOutput, calls=%fused_computation.25 | convolution fusion | flops 536870912 | bytes 5505028 | tf_op jit(solution)/shard_map/dot_general | solution.py:179
  81.6 0.0 copy-done.3
  81.6 3.1 %fusion = bf16[1,512,2048]{2,1,0:T(8,128)(2,1)} fusion(f32[512,2048]{1,0:T(8,128)S(1)} %fusion.14, s32[512]{0:T(512)S(1)} %copy-done.3, bf16[2048,128]{1,0:T(8,128)(2,1)S(1)} %squeeze.6, bf16[2048,128]{1,0:T(8,128)(2,1)S(1)} %get-tuple-element.7, bf16[2048,256]{1,0:T(8,128)(2,1)} %get-tuple-element.8, s32[]{:T(128)S(6)} %select_n.46), kind=kOutput, calls=%fused_computation.5 | convolution fusion | flops 543162368 | bytes 7604228 | tf_op jit(solution)/shard_map/dot_general | solution.py:180
  (3 shorter events, 0.1 us)
Async XLA Ops:
  0.0 9.8 %copy-start.1 = (bf16[3,16,2048]{2,1,0:T(8,128)(2,1)S(1)}, bf16[3,16,2048]{2,1,0:T(8,128)(2,1)}, u32[]{:S(2)}) copy-start(bf16[3,16,2048]{2,1,0:T(8,128)(2,1)} %param.5) | copy-start | bytes 589828
  1.0 8.8 %collective-permute-start = (bf16[3,16,2048]{2,1,0:T(8,128)(2,1)S(1)}, bf16[3,16,2048]{2,1,0:T(8,128)(2,1)}, u32[]{:S(2)}, u32[]{:S(2)}) collective-permute-start(bf16[3,16,2048]{2,1,0:T(8,128)(2,1)S(1)} %slice.33), channel_id=1, source_target_pairs={{0,1},{1,2},{2,3},{4,5},{5,6},{6,7},{8,9},{9,10},{10,11},{12,13},{... | collective-permute-start | bytes 589832 | tf_op jit(solution)/shard_map/ppermute | solution.py:150
  7.5 2.3 %copy-start = (bf16[32,16,2048]{2,1,0:T(8,128)(2,1)S(1)}, bf16[32,16,2048]{2,1,0:T(8,128)(2,1)}, u32[]{:S(2)}) copy-start(bf16[32,16,2048]{2,1,0:T(8,128)(2,1)} %param.4) | copy-start | bytes 6291460
  7.6 1.0 %copy-start.2 = (f32[4,2048]{1,0:T(4,128)S(1)}, f32[4,2048]{1,0:T(4,128)}, u32[]{:S(2)}) copy-start(f32[4,2048]{1,0:T(4,128)} %param.6) | copy-start | bytes 98308
  79.5 2.1 %copy-start.3 = (s32[512]{0:T(512)S(1)}, s32[512]{0:T(512)}, u32[]{:S(2)}) copy-start(s32[512]{0:T(512)} %iota_add_fusion) | copy-start | bytes 6148

commit v2 on v1

v2 whole, which is shorter than its diff:
```python
import functools
import math

import jax
import jax.numpy as jnp
from jax import lax
from jax.experimental import pallas as pl
from jax.experimental.pallas import tpu as pltpu
from jax.sharding import PartitionSpec as P

TAPS = 4
SAMPLES, FRAMES, ROWS = 2048, 32, 512
MESH = pl.DeviceIdType.MESH
NI, NV, NY, NZ = 128, 4, 8, 8
ZGROUPS = ((0,), (1, 7), (2, 6), (3, 5), (4,))
DEPTH = 1


def trig(m):
    quadrant = (m + 256) >> 9
    x = (m - (quadrant << 9)).astype(jnp.float32) * (2.0 * math.pi / SAMPLES)
    s = x * x
    c = 1.0 + s * (-0.5 + s * (1.0 / 24 + s * (-1.0 / 720 + s * (1.0 / 40320))))
    d = x * (1.0 + s * (-1.0 / 6 + s * (1.0 / 120 + s * (-1.0 / 5040 + s * (1.0 / 362880)))))
    odd = (quadrant & 1) == 1
    cos = jnp.where(odd, d, c)
    sin = jnp.where(odd, c, d)
    cos = jnp.where((quadrant == 1) | (quadrant == 2), -cos, cos)
    sin = jnp.where((quadrant == 2) | (quadrant == 3), -sin, sin)
    return cos, sin


def write_table(kept_ref, table_ref):
    lane = lax.broadcasted_iota(jnp.int32, (NI, 128), 1)
    here = lane == lax.broadcasted_iota(jnp.int32, (NI, 128), 0)
    kept = jnp.broadcast_to(kept_ref[...], (NI, 128)).astype(jnp.float32)
    kept = jnp.sum(jnp.where(here, kept, 0.0), axis=1, keepdims=True).astype(jnp.int32)
    cl, sl = trig((kept * lane) & (SAMPLES - 1))
    ch, sh = trig((kept * lane * 128) & (SAMPLES - 1))
    scale = 1.0 / math.sqrt(SAMPLES)
    cl, sl = cl * scale, sl * scale
    for high in range(SAMPLES // 128):
        a = jnp.broadcast_to(ch[:, high : high + 1], (NI, 128))
        b = jnp.broadcast_to(sh[:, high : high + 1], (NI, 128))
        cols = slice(high * 128, high * 128 + 128)
        table_ref[0:NI, cols] = (a * cl - b * sl).astype(jnp.bfloat16)
        table_ref[NI:, cols] = (-(b * cl) - a * sl).astype(jnp.bfloat16)


def write_order(order_ref):
    m = lax.broadcasted_iota(jnp.int32, (512, 512), 0)
    t = lax.broadcasted_iota(jnp.int32, (512, 512), 1)
    source = ((t & 31) << 4) | (((t >> 6) & 1) << 3) | ((t >> 7) << 1) | ((t >> 5) & 1)
    order_ref[...] = jnp.where(m == source, 1.0, 0.0).astype(jnp.bfloat16)


def filter_frames(source_ref, previous_ref, taps_ref, weighted_ref, first, last, lo, hi):
    def chunk(j, _):
        cols = pl.ds(pl.multiple_of(j * 128, 128), 128)
        taps = [jnp.broadcast_to(taps_ref[t : t + 1, cols], (16, 128)) for t in range(TAPS)]
        window = [previous_ref[k, :, cols].astype(jnp.float32) for k in range(TAPS - 1)]
        for f in range(first, last):
            window.append(source_ref[f, :, cols].astype(jnp.float32))
            total = taps[0] * window[0]
            for t in range(1, TAPS):
                total = total + taps[t] * window[t]
            weighted_ref[f * 16 : f * 16 + 16, cols] = total.astype(jnp.bfloat16)
            window = window[1:]
        return 0

    lax.fori_loop(lo, hi, chunk, 0)


def write_blocks(table_ref, weighted_ref, order_ref, wide_ref, z_ref):
    nt = (((1,), (1,)), ((), ()))
    spectra = lax.dot_general(table_ref[...], weighted_ref[...], nt, preferred_element_type=jnp.float32)
    spectra = spectra.astype(jnp.bfloat16)
    spectra = jnp.dot(spectra, order_ref[...], preferred_element_type=jnp.float32)
    even = (lax.broadcasted_iota(jnp.int32, (NI, 128), 1) & 32) == 0
    for pair in range(4):
        cols = slice(pair * 128, pair * 128 + 128)
        re, im = spectra[0:NI, cols], spectra[NI:, cols]
        wide_ref[pl.ds(2 * pair, NI, stride=8), :] = jnp.where(even, re, pltpu.roll(im, 32, 1))
        wide_ref[pl.ds(2 * pair + 1, NI, stride=8), :] = jnp.where(even, pltpu.roll(re, 96, 1), im)
    z_ref[...] = wide_ref[...].reshape(NI, 8, 128).astype(jnp.bfloat16)


def correlate_kernel(g_ref, out_ref, all_ref, re_ref, im_ref):
    j = pl.program_id(0)
    v = lax.axis_index("vis")

    @pl.when(j == 0)
    def _():
        first = lax.broadcasted_iota(jnp.int32, (128, 16, 128), 2) < 64
        low = lax.broadcasted_iota(jnp.int32, (128, 8, 128), 2) < 64
        for pair in range(2):
            a = g_ref[2 * pair].astype(jnp.float32)
            b = g_ref[2 * pair + 1].astype(jnp.float32)
            top = jnp.where(low, a, pltpu.roll(b, 64, 2))
            bottom = jnp.where(low, pltpu.roll(a, 64, 2), b)
            rows = jnp.concatenate([top, bottom], axis=1).reshape(2048, 128)
            all_ref[:, pair * 128 : pair * 128 + 128] = rows.astype(jnp.bfloat16)
        own = all_ref[pl.ds(pl.multiple_of(v * ROWS, ROWS), ROWS), :].astype(jnp.float32)
        re_ref[...] = own.astype(jnp.bfloat16)
        real = (lax.broadcasted_iota(jnp.int32, (ROWS, 128), 1) & 32) == 0
        for pair in range(2):
            x = own[:, pair * 128 : pair * 128 + 128]
            turned = jnp.where(real, pltpu.roll(x, 96, 1), -pltpu.roll(x, 32, 1))
            im_ref[:, pair * 128 : pair * 128 + 128] = turned.astype(jnp.bfloat16)

    nt = (((1,), (1,)), ((), ()))
    cols = all_ref[pl.ds(pl.multiple_of(j * ROWS, ROWS), ROWS), :]
    scale = 1.0 / (NV * FRAMES)

    @pl.when(j > v)
    def _():
        out_ref[0] = (lax.dot_general(re_ref[...], cols, nt, preferred_element_type=jnp.float32) * scale).astype(jnp.bfloat16)

    @pl.when(j < v)
    def _():
        out_ref[0] = (lax.dot_general(im_ref[...], cols, nt, preferred_element_type=jnp.float32) * scale).astype(jnp.bfloat16)

    @pl.when(j == v)
    def _():
        re = lax.dot_general(re_ref[...], cols, nt, preferred_element_type=jnp.float32)
        im = lax.dot_general(im_ref[...], cols, nt, preferred_element_type=jnp.float32)
        row = lax.broadcasted_iota(jnp.int32, (ROWS, ROWS), 0)
        col = lax.broadcasted_iota(jnp.int32, (ROWS, ROWS), 1)
        out_ref[0] = (jnp.where(col >= row, re, im) * scale).astype(jnp.bfloat16)


def correlate(gathered):
    return pl.pallas_call(
        correlate_kernel,
        grid=(NV,),
        out_shape=jax.ShapeDtypeStruct((1, ROWS, NV * ROWS), jnp.bfloat16),
        in_specs=[pl.BlockSpec((NV, NI, 8, 128), lambda j: (0, 0, 0, 0))],
        out_specs=pl.BlockSpec((1, ROWS, ROWS), lambda j: (0, 0, j)),
        scratch_shapes=[
            pltpu.VMEM((NV * ROWS, 256), jnp.bfloat16),
            pltpu.VMEM((ROWS, 256), jnp.bfloat16),
            pltpu.VMEM((ROWS, 256), jnp.bfloat16),
        ],
    )(gathered)


def channelize_kernel(
    samples_ref, history_ref, taps_ref, kept_ref, g_ref,
    frames_ref, previous_ref, table_ref, weighted_ref, order_ref, wide_ref, z_ref,
    load_sem, h_send, h_recv, gossip, a_send, a_recv, x_send, x_recv,
):
    me = lax.axis_index("inp")
    v = lax.axis_index("vis")
    y, z, c = me // 16, lax.rem(me // 2, 8), lax.rem(me, 2)
    right, left, opp = lax.rem(v + 1, NV), lax.rem(v + 3, NV), lax.rem(v + 2, NV)

    def place(dy, dz, dc):
        return lax.rem(y + dy, 8) * 16 + lax.rem(z + dz, 8) * 2 + lax.rem(c + dc, 2)

    barrier = pltpu.get_barrier_semaphore()
    for step in ((1, 0, 0), (7, 0, 0), (0, 1, 0), (0, 7, 0), (0, 0, 1)):
        pl.semaphore_signal(barrier, inc=1, device_id=(place(*step), v), device_id_type=MESH)
    for other in (left, right):
        pl.semaphore_signal(barrier, inc=1, device_id=(me, other), device_id_type=MESH)
    load = pltpu.make_async_copy(samples_ref, frames_ref, load_sem.at[0])
    load.start()
    write_table(kept_ref, table_ref)
    pl.semaphore_wait(barrier, 7)

    tail = samples_ref.at[pl.ds(FRAMES - TAPS + 1, TAPS - 1)]
    handover = pltpu.make_async_remote_copy(
        src_ref=tail, dst_ref=previous_ref, send_sem=h_send, recv_sem=h_recv, device_id=(me, right), device_id_type=MESH
    )
    own_history = pltpu.make_async_copy(history_ref, previous_ref, load_sem.at[1])

    @pl.when(v < NV - 1)
    def _():
        handover.start()

    @pl.when(v == 0)
    def _():
        own_history.start()

    def tell(k, *step):
        pl.semaphore_signal(gossip.at[k], inc=1, device_id=(place(*step), v), device_id_type=MESH)

    def hear(*ks):
        for k in ks:
            pl.semaphore_wait(gossip.at[k], 1)

    def tell_y():
        tell(0, 1, 0, 0)
        tell(1, 7, 0, 0)

    def tell_z():
        tell(2, 0, 1, 0)
        tell(3, 0, 7, 0)

    tell_y()
    write_order(order_ref)
    load.wait()

    def filter_part(lo, hi):
        filter_frames(frames_ref, frames_ref, taps_ref, weighted_ref, TAPS - 1, FRAMES, lo, hi)

    hear(0, 1)
    tell_y()
    filter_part(0, 4)
    hear(0, 1)
    tell_y()
    filter_part(4, 8)
    hear(0, 1)
    tell(4, 0, 0, 1)
    filter_part(8, 12)
    hear(4)
    tell_z()
    filter_part(12, 16)

    @pl.when(v == 0)
    def _():
        own_history.wait()

    @pl.when(v > 0)
    def _():
        handover.wait_recv()

    filter_frames(frames_ref, previous_ref, taps_ref, weighted_ref, 0, TAPS - 1, 0, 16)
    write_blocks(table_ref, weighted_ref, order_ref, wide_ref, z_ref)

    @pl.when(v < NV - 1)
    def _():
        handover.wait_send()

    own = pltpu.make_async_copy(z_ref.at[me], g_ref.at[v, y, z, c], load_sem.at[2])
    own.start()

    def send(dy, dz, dc):
        target = place(dy, dz, dc)
        pltpu.make_async_remote_copy(
            src_ref=z_ref.at[target],
            dst_ref=g_ref.at[v, y, z, c],
            send_sem=a_send,
            recv_sem=a_recv.at[(8 - dz) % 8],
            device_id=(target, v),
            device_id_type=MESH,
        ).start()

    for k, group in enumerate(ZGROUPS):
        if k == 0:
            send(0, 0, 1)
        else:
            hear(2, 3)
            if k < 4:
                tell_z()

        def body(dy, _, group=group):
            for dc in (0, 1):
                for dz in group:
                    send(dy, dz, dc)
            return 0

        lax.fori_loop(1 if k == 0 else 0, 8, body, 0)
    own.wait()

    def whole(vv, tz):
        return g_ref.at[vv, :, tz]

    def half(vv, tz, h):
        return g_ref.at[vv, pl.ds(4 * h, 4), tz]

    def relay(k):
        for dz in ZGROUPS[k]:
            tz = lax.rem(z + dz, 8)
            for side, (source, target) in enumerate(((left, right), (right, left))):
                pltpu.make_async_copy(whole(source, tz), whole(source, tz), x_recv.at[dz, side]).wait()
                pltpu.make_async_remote_copy(
                    src_ref=half(source, tz, side),
                    dst_ref=half(source, tz, side),
                    send_sem=x_send.at[2],
                    recv_sem=x_recv.at[dz, 2 + side],
                    device_id=(me, target),
                    device_id_type=MESH,
                ).start()

    for k, group in enumerate(ZGROUPS):
        for dz in group:
            tz = lax.rem(z + dz, 8)
            if dz == 0:
                pltpu.make_async_copy(z_ref.at[pl.ds(0, 15)], z_ref.at[pl.ds(0, 15)], a_recv.at[0]).wait()
            else:
                pltpu.make_async_copy(whole(v, tz), whole(v, tz), a_recv.at[dz]).wait()
            for side, target in enumerate((right, left)):
                pltpu.make_async_remote_copy(
                    src_ref=whole(v, tz),
                    dst_ref=whole(v, tz),
                    send_sem=x_send.at[side],
                    recv_sem=x_recv.at[dz, side],
                    device_id=(me, target),
                    device_id_type=MESH,
                ).start()
        if k >= DEPTH:
            relay(k - DEPTH)
    for k in range(len(ZGROUPS) - DEPTH, len(ZGROUPS)):
        relay(k)
    for dz in range(8):
        tz = lax.rem(z + dz, 8)
        for side in range(2):
            pltpu.make_async_copy(half(opp, tz, side), half(opp, tz, side), x_recv.at[dz, 2 + side]).wait()
    for i in range(3):
        pltpu.make_async_copy(g_ref.at[v], g_ref.at[v], x_send.at[i]).wait()
    pltpu.make_async_copy(z_ref.at[pl.ds(0, NI - 1)], z_ref.at[pl.ds(0, NI - 1)], a_send).wait()


def channelize(samples, history, fir_taps, kept_channels):
    vmem = pl.BlockSpec(memory_space=pltpu.VMEM)
    hbm = pl.BlockSpec(memory_space=pl.ANY)
    return pl.pallas_call(
        channelize_kernel,
        out_shape=jax.ShapeDtypeStruct((NV, NY, NZ, 2, 8, 128), jnp.bfloat16),
        in_specs=[hbm, hbm, vmem, vmem],
        out_specs=vmem,
        scratch_shapes=[
            pltpu.VMEM((FRAMES, 16, SAMPLES), jnp.bfloat16),
            pltpu.VMEM((TAPS - 1, 16, SAMPLES), jnp.bfloat16),
            pltpu.VMEM((2 * NI, SAMPLES), jnp.bfloat16),
            pltpu.VMEM((512, SAMPLES), jnp.bfloat16),
            pltpu.VMEM((512, 512), jnp.bfloat16),
            pltpu.VMEM((1024, 128), jnp.float32),
            pltpu.VMEM((NI, 8, 128), jnp.bfloat16),
            pltpu.SemaphoreType.DMA((3,)),
            pltpu.SemaphoreType.DMA,
            pltpu.SemaphoreType.DMA,
            pltpu.SemaphoreType.REGULAR((5,)),
            pltpu.SemaphoreType.DMA,
            pltpu.SemaphoreType.DMA((8,)),
            pltpu.SemaphoreType.DMA((3,)),
            pltpu.SemaphoreType.DMA((8, 4)),
        ],
        compiler_params=pltpu.CompilerParams(collective_id=0, has_side_effects=True),
    )(samples, history, fir_taps, kept_channels.reshape(1, NI))


def per_device(samples, history, fir_taps, kept_channels):
    gathered = channelize(samples, history, fir_taps, kept_channels)
    return correlate(gathered.reshape(NV, NI, 8, 128))


def solution(mesh):
    return jax.shard_map(
        per_device,
        mesh=mesh,
        in_specs=(P("vis", "inp", None), P(None, "inp", None), P(), P()),
        out_specs=P("inp", "vis", None),
        check_vma=False,
    )
```

time: 85.5 us -> 46.5 us (0.54)
  local copies, waits for them, and re-layouts: 28.6 us -> 0 us
  Pallas kernels: 37.7 us -> 45.6 us
  matrix products: 6.84 us -> 0 us
  other arithmetic: 6.81 us -> 0 us
  starting transfers between devices: 4.63 us -> 0 us
    slice x5 -> x0, local copies, waits for them, and re-layouts: 14.2 us -> none  [the longest x3 12.6 us: per_device(): real, imag = (parts[0], parts[1])]
    reshape x4 -> x0, local copies, waits for them, and re-layouts: 10.7 us -> none  [the longest x1 9.74 us: per_device(): gathered = gathered.reshape(NV, NI, 8, 2, 2, frame_count)]
    pallas_call x1 -> x2, Pallas kernels: 37.7 us -> 45.6 us  [the longest x1 40.9 us: channelize(): pl.pallas_call(channelize_kernel, out_shape=jax.ShapeDtypeStruct((NV, NY,...]
    dot_general x3 -> x0, matrix products: 6.84 us -> none  [the longest x1 3.14 us: per_device(): lax.dot_general(block, turned, dims, preferred_element_type=jnp.float32)]
    ppermute x1 -> x0, starting transfers between devices: 4.63 us -> none  [shifted(): lax.ppermute(value, axis, [(source, source + steps) for source in range(i...]
    convert_element_type x1 -> x0, other arithmetic: 2.74 us -> none  [per_device(): weighted = weighted.astype(jnp.bfloat16)]
    squeeze x2 -> x0, local copies, waits for them, and re-layouts: 2.29 us -> none  [per_device(): real, imag = (parts[0], parts[1])]
    mul x2 -> x0, other arithmetic: 1 us -> none  [the longest x1 0.99 us: make_table(): cl, sl = ((cl * scale)[:, None, :], (sl * scale)[:, None, :])]
  transfers between devices with their start and end apart: 1 -> 0, of which waited for: 0 -> 0; matrix products, arithmetic and copies ran while one was open for 5% -> 0% of each run, Pallas kernels for 0% -> 0%
where the time goes in v2:
time: 46.5 us; the launch traced here: 45.6 us
  Pallas kernels  45.6 us (98%)
    pallas_call x1, Pallas kernels, channelize(): pl.pallas_call(channelize_kernel, out_shape=jax.ShapeDtypeStruct((NV, NY,...  40.9 us
    pallas_call x1, Pallas kernels, correlate(): pl.pallas_call(correlate_kernel, grid=(NV,), out_shape=jax.ShapeDtypeStru...  4.72 us

profile of v2, /device:TPU:1, one launch (start us, length us, event | category | flops | bytes accessed | tf_op | source)
XLA Modules:
  0.0 45.6 jit_solution(3581667329062789306)
XLA Ops:
  0.0 40.9 %shard_map.46 = bf16[4,8,8,2,8,128]{5,4,3,2,1,0:T(8,128)(2,1)} custom-call(bf16[32,16,2048]{2,1,0:T(8,128)(2,1)} %samples_ref.1, bf16[3,16,2048]{2,1,0:T(8,128)(2,1)} %history_ref.1, f32[4,2048]{1,0:T(4,128)} %taps_ref.1, s32[1,128]{1,0:T(1,128)} %bitcast.3), custom_call_target="tpu_custom_call" | custom-call | tf_op jit(solution)/shard_map/pallas_call | solution.py:317
  40.9 4.7 %shard_map.47 = bf16[1,512,2048]{2,1,0:T(8,128)(2,1)} custom-call(bf16[4,128,8,128]{3,2,1,0:T(8,128)(2,1)} %bitcast.2), custom_call_target="tpu_custom_call" | custom-call | tf_op jit(solution)/shard_map/pallas_call | solution.py:133

commit v3 on v2

v3 whole, which is shorter than its diff:
```python
import functools
import math

import jax
import jax.numpy as jnp
from jax import lax
from jax.experimental import pallas as pl
from jax.experimental.pallas import tpu as pltpu
from jax.sharding import PartitionSpec as P

TAPS = 4
SAMPLES, FRAMES, ROWS = 2048, 32, 512
MESH = pl.DeviceIdType.MESH
NI, NV, NY, NZ = 128, 4, 8, 8
ZGROUPS = ((0,), (1, 7), (2, 6), (3, 5), (4,))
DEPTH = 1
DIRECT = (0, 1, 2, 3, 4, 5, 6, 7)


def trig(m):
    quadrant = (m + 256) >> 9
    x = (m - (quadrant << 9)).astype(jnp.float32) * (2.0 * math.pi / SAMPLES)
    s = x * x
    c = 1.0 + s * (-0.5 + s * (1.0 / 24 + s * (-1.0 / 720 + s * (1.0 / 40320))))
    d = x * (1.0 + s * (-1.0 / 6 + s * (1.0 / 120 + s * (-1.0 / 5040 + s * (1.0 / 362880)))))
    odd = (quadrant & 1) == 1
    cos = jnp.where(odd, d, c)
    sin = jnp.where(odd, c, d)
    cos = jnp.where((quadrant == 1) | (quadrant == 2), -cos, cos)
    sin = jnp.where((quadrant == 2) | (quadrant == 3), -sin, sin)
    return cos, sin


def write_table(kept_ref, table_ref):
    lane = lax.broadcasted_iota(jnp.int32, (NI, 128), 1)
    here = lane == lax.broadcasted_iota(jnp.int32, (NI, 128), 0)
    kept = jnp.broadcast_to(kept_ref[...], (NI, 128)).astype(jnp.float32)
    kept = jnp.sum(jnp.where(here, kept, 0.0), axis=1, keepdims=True).astype(jnp.int32)
    cl, sl = trig((kept * lane) & (SAMPLES - 1))
    ch, sh = trig((kept * lane * 128) & (SAMPLES - 1))
    scale = 1.0 / math.sqrt(SAMPLES)
    cl, sl = cl * scale, sl * scale
    for high in range(SAMPLES // 128):
        a = jnp.broadcast_to(ch[:, high : high + 1], (NI, 128))
        b = jnp.broadcast_to(sh[:, high : high + 1], (NI, 128))
        cols = slice(high * 128, high * 128 + 128)
        table_ref[0:NI, cols] = (a * cl - b * sl).astype(jnp.bfloat16)
        table_ref[NI:, cols] = (-(b * cl) - a * sl).astype(jnp.bfloat16)


def write_order(order_ref):
    m = lax.broadcasted_iota(jnp.int32, (512, 512), 0)
    t = lax.broadcasted_iota(jnp.int32, (512, 512), 1)
    source = ((t & 31) << 4) | (((t >> 6) & 1) << 3) | ((t >> 7) << 1) | ((t >> 5) & 1)
    order_ref[...] = jnp.where(m == source, 1.0, 0.0).astype(jnp.bfloat16)


def filter_frames(source_ref, taps_ref, weighted_ref, lo, hi):
    def chunk(j, _):
        cols = pl.ds(pl.multiple_of(j * 128, 128), 128)
        taps = [jnp.broadcast_to(taps_ref[t : t + 1, cols], (16, 128)) for t in range(TAPS)]
        window = []
        for f in range(FRAMES):
            window.append(source_ref[f, :, cols].astype(jnp.float32))
            window = window[-TAPS:]
            terms = taps[TAPS - len(window) :]
            total = terms[0] * window[0]
            for t in range(1, len(window)):
                total = total + terms[t] * window[t]
            weighted_ref[f * 16 : f * 16 + 16, cols] = total.astype(jnp.bfloat16)
        return 0

    lax.fori_loop(lo, hi, chunk, 0)


def write_tail(last, taps_ref, table_ref, spill_ref, tail_ref):
    def chunk(j, _):
        cols = pl.ds(pl.multiple_of(j * 128, 128), 128)
        taps = [jnp.broadcast_to(taps_ref[t : t + 1, cols], (16, 128)) for t in range(TAPS - 1)]
        window = [last(k, cols).astype(jnp.float32) for k in range(TAPS - 1)]
        for f in range(TAPS - 1):
            total = taps[0] * window[f]
            for t in range(1, TAPS - 1 - f):
                total = total + taps[t] * window[f + t]
            spill_ref[f * 16 : f * 16 + 16, cols] = total.astype(jnp.bfloat16)
        return 0

    lax.fori_loop(0, SAMPLES // 128, chunk, 0)
    nt = (((1,), (1,)), ((), ()))
    tail = lax.dot_general(spill_ref[...], table_ref[...], nt, preferred_element_type=jnp.float32)
    tail_ref[...] = tail.astype(jnp.bfloat16)


def write_blocks(table_ref, weighted_ref, head_ref, order_ref, wide_ref, z_ref):
    nt = (((1,), (1,)), ((), ()))
    spectra = lax.dot_general(table_ref[...], weighted_ref[...], nt, preferred_element_type=jnp.float32)
    count = (TAPS - 1) * 16
    place = lax.broadcasted_iota(jnp.int32, (count, 128), 0) == lax.broadcasted_iota(jnp.int32, (count, 128), 1)
    place = jnp.where(place, 1.0, 0.0).astype(jnp.bfloat16)
    tn = (((0,), (0,)), ((), ()))
    first = spectra[:, 0:128] + lax.dot_general(head_ref[...], place, tn, preferred_element_type=jnp.float32)
    spectra = jnp.concatenate([first, spectra[:, 128:]], axis=1).astype(jnp.bfloat16)
    spectra = jnp.dot(spectra, order_ref[...], preferred_element_type=jnp.float32)
    even = (lax.broadcasted_iota(jnp.int32, (NI, 128), 1) & 32) == 0
    for pair in range(4):
        cols = slice(pair * 128, pair * 128 + 128)
        re, im = spectra[0:NI, cols], spectra[NI:, cols]
        wide_ref[pl.ds(2 * pair, NI, stride=8), :] = jnp.where(even, re, pltpu.roll(im, 32, 1))
        wide_ref[pl.ds(2 * pair + 1, NI, stride=8), :] = jnp.where(even, pltpu.roll(re, 96, 1), im)
    z_ref[...] = wide_ref[...].reshape(NI, 8, 128).astype(jnp.bfloat16)


def correlate_kernel(rows_ref, out_ref, im_ref, stage_ref, sem):
    v = lax.axis_index("vis")
    own = rows_ref.at[pl.ds(pl.multiple_of(v * ROWS, ROWS), ROWS)]
    real = (lax.broadcasted_iota(jnp.int32, (ROWS, 128), 1) & 32) == 0
    for pair in range(2):
        x = own[:, pair * 128 : pair * 128 + 128].astype(jnp.float32)
        turned = jnp.where(real, pltpu.roll(x, 96, 1), -pltpu.roll(x, 32, 1))
        im_ref[:, pair * 128 : pair * 128 + 128] = turned.astype(jnp.bfloat16)

    nt = (((1,), (1,)), ((), ()))
    scale = 1.0 / (NV * FRAMES)
    for j in range(NV):
        cols = slice(j * ROWS, j * ROWS + ROWS)

        def product(ref, cols=cols):
            return lax.dot_general(ref[...], rows_ref[cols, :], nt, preferred_element_type=jnp.float32) * scale

        @pl.when(v < j)
        def _():
            stage_ref[j] = product(own).astype(jnp.bfloat16)

        @pl.when(v > j)
        def _():
            stage_ref[j] = product(im_ref).astype(jnp.bfloat16)

        @pl.when(v == j)
        def _():
            row = lax.broadcasted_iota(jnp.int32, (ROWS, ROWS), 0)
            col = lax.broadcasted_iota(jnp.int32, (ROWS, ROWS), 1)
            stage_ref[j] = jnp.where(col >= row, product(own), product(im_ref)).astype(jnp.bfloat16)

        pltpu.make_async_copy(stage_ref.at[j], out_ref.at[0, :, pl.ds(j * ROWS, ROWS)], sem.at[j]).start()
    for j in range(NV):
        pltpu.make_async_copy(stage_ref.at[j], out_ref.at[0, :, pl.ds(j * ROWS, ROWS)], sem.at[j]).wait()


def correlate(rows):
    return pl.pallas_call(
        correlate_kernel,
        out_shape=jax.ShapeDtypeStruct((1, ROWS, NV * ROWS), jnp.bfloat16),
        in_specs=[pl.BlockSpec(memory_space=pltpu.VMEM)],
        out_specs=pl.BlockSpec(memory_space=pl.ANY),
        scratch_shapes=[
            pltpu.VMEM((ROWS, 256), jnp.bfloat16),
            pltpu.VMEM((NV, ROWS, ROWS), jnp.bfloat16),
            pltpu.SemaphoreType.DMA((NV,)),
        ],
    )(rows)


def channelize_kernel(
    samples_ref, history_ref, taps_ref, kept_ref, out_ref,
    frames_ref, previous_ref, table_ref, weighted_ref, order_ref, wide_ref, z_ref, g_ref, stage_ref, spill_ref, tail_ref, head_ref,
    load_sem, h_send, h_recv, gossip, a_send, a_recv, x_send, x_recv, out_sem,
):
    me = lax.axis_index("inp")
    v = lax.axis_index("vis")
    y, z, c = me // 16, lax.rem(me // 2, 8), lax.rem(me, 2)
    right, left, opp = lax.rem(v + 1, NV), lax.rem(v + 3, NV), lax.rem(v + 2, NV)

    def place(dy, dz, dc):
        return lax.rem(y + dy, 8) * 16 + lax.rem(z + dz, 8) * 2 + lax.rem(c + dc, 2)

    barrier = pltpu.get_barrier_semaphore()

    def greet(dy, _):
        for dc in (0, 1):
            pl.semaphore_signal(barrier, inc=1, device_id=(place(dy, 0, dc), v), device_id_type=MESH)
        return 0

    lax.fori_loop(1, NY, greet, 0)
    for step in ((0, 0, 1), (0, 1, 0), (0, 7, 0)):
        pl.semaphore_signal(barrier, inc=1, device_id=(place(*step), v), device_id_type=MESH)
    for other in (left, right, opp):
        pl.semaphore_signal(barrier, inc=1, device_id=(me, other), device_id_type=MESH)

    load = pltpu.make_async_copy(samples_ref, frames_ref, load_sem.at[0])
    load.start()
    old = pltpu.make_async_copy(history_ref, previous_ref, load_sem.at[1])
    old.start()
    write_order(order_ref)
    write_table(kept_ref, table_ref)
    def tell_z():
        pl.semaphore_signal(gossip.at[0], inc=1, device_id=(place(0, 1, 0), v), device_id_type=MESH)
        pl.semaphore_signal(gossip.at[1], inc=1, device_id=(place(0, 7, 0), v), device_id_type=MESH)

    def hear_z():
        pl.semaphore_wait(gossip.at[0], 1)
        pl.semaphore_wait(gossip.at[1], 1)

    load.wait()
    write_tail(lambda k, cols: frames_ref[FRAMES - TAPS + 1 + k, :, cols], taps_ref, table_ref, spill_ref, tail_ref)
    old.wait()

    @pl.when(v == 0)
    def _():
        write_tail(lambda k, cols: previous_ref[k, :, cols], taps_ref, table_ref, spill_ref, head_ref)

    handover = pltpu.make_async_remote_copy(
        src_ref=tail_ref, dst_ref=head_ref, send_sem=h_send, recv_sem=h_recv, device_id=(me, right), device_id_type=MESH
    )

    filter_frames(frames_ref, taps_ref, weighted_ref, 0, 4)
    pl.semaphore_wait(barrier, 2 * (NY - 1) + 6)
    tell_z()

    @pl.when(v < NV - 1)
    def _():
        handover.start()

    filter_frames(frames_ref, taps_ref, weighted_ref, 4, 16)

    @pl.when(v > 0)
    def _():
        handover.wait_recv()

    write_blocks(table_ref, weighted_ref, head_ref, order_ref, wide_ref, z_ref)

    @pl.when(v < NV - 1)
    def _():
        handover.wait_send()
    own = pltpu.make_async_copy(z_ref.at[me], g_ref.at[v, y, z, c], load_sem.at[2])
    own.start()

    def send(target, dz):
        pltpu.make_async_remote_copy(
            src_ref=z_ref.at[target],
            dst_ref=g_ref.at[v, y, z, c],
            send_sem=a_send,
            recv_sem=a_recv.at[(8 - dz) % 8],
            device_id=(target, v),
            device_id_type=MESH,
        ).start()

    for k, group in enumerate(ZGROUPS):
        bases = [(dz, lax.rem(z + dz, NZ) * 2) for dz in group]
        if k == 0:
            send(place(0, 0, 1), 0)
        else:
            hear_z()
            if k < 4:
                tell_z()

        def body(i, _, bases=bases):
            row = lax.rem(y + 8 + (i + 1) // 2 * (2 * lax.rem(i, 2) - 1), NY) * 16
            for core in (0, 1):
                for dz, base in bases:
                    send(row + base + core, dz)
            return 0

        lax.fori_loop(1 if k == 0 else 0, NY, body, 0)
    own.wait()

    def whole(vv, tz):
        return g_ref.at[vv, :, tz]

    def half(vv, tz, h):
        return g_ref.at[vv, pl.ds(4 * h, 4), tz]

    def relay(k):
        for dz in ZGROUPS[k]:
            if dz in DIRECT:
                continue
            tz = lax.rem(z + dz, 8)
            for side, (source, target) in enumerate(((left, right), (right, left))):
                pltpu.make_async_copy(whole(source, tz), whole(source, tz), x_recv.at[dz, side]).wait()
                pltpu.make_async_remote_copy(
                    src_ref=half(source, tz, side),
                    dst_ref=half(source, tz, side),
                    send_sem=x_send.at[2],
                    recv_sem=x_recv.at[dz, 2 + side],
                    device_id=(me, target),
                    device_id_type=MESH,
                ).start()

    for k, group in enumerate(ZGROUPS):
        for dz in group:
            tz = lax.rem(z + dz, 8)
            if dz == 0:
                pltpu.make_async_copy(z_ref.at[pl.ds(0, 15)], z_ref.at[pl.ds(0, 15)], a_recv.at[0]).wait()
            else:
                pltpu.make_async_copy(whole(v, tz), whole(v, tz), a_recv.at[dz]).wait()
            for side, target in enumerate((right, left)):
                pltpu.make_async_remote_copy(
                    src_ref=whole(v, tz),
                    dst_ref=whole(v, tz),
                    send_sem=x_send.at[side],
                    recv_sem=x_recv.at[dz, side],
                    device_id=(me, target),
                    device_id_type=MESH,
                ).start()
            if dz in DIRECT:
                pltpu.make_async_remote_copy(
                    src_ref=whole(v, tz),
                    dst_ref=whole(v, tz),
                    send_sem=x_send.at[2],
                    recv_sem=x_recv.at[dz, 2],
                    device_id=(me, opp),
                    device_id_type=MESH,
                ).start()
        if k >= DEPTH:
            relay(k - DEPTH)
    for k in range(len(ZGROUPS) - DEPTH, len(ZGROUPS)):
        relay(k)
    low = lax.broadcasted_iota(jnp.int32, (2, 8, 128), 2) < 64
    for k, dz in enumerate(dz for group in ZGROUPS for dz in group):
        tz = lax.rem(z + dz, 8)
        if dz in DIRECT:
            for side, source in enumerate((left, right, opp)):
                pltpu.make_async_copy(whole(source, tz), whole(source, tz), x_recv.at[dz, side]).wait()
        else:
            for side in range(2):
                pltpu.make_async_copy(half(opp, tz, side), half(opp, tz, side), x_recv.at[dz, 2 + side]).wait()

        def rows(row, _, k=k, tz=tz):
            for pair in range(2):
                p = g_ref[2 * pair, row, tz].astype(jnp.float32)
                q = g_ref[2 * pair + 1, row, tz].astype(jnp.float32)
                top = jnp.where(low, p, pltpu.roll(q, 64, 2))
                bottom = jnp.where(low, pltpu.roll(p, 64, 2), q)
                both = jnp.concatenate([top, bottom], axis=1).reshape(32, 128)
                stage_ref[k, row, :, pair * 128 : pair * 128 + 128] = both.astype(jnp.bfloat16)
            return 0

        lax.fori_loop(0, NY, rows, 0)
        pltpu.make_async_copy(stage_ref.at[k], out_ref.at[:, tz], out_sem).start()
    pltpu.make_async_copy(stage_ref, out_ref, out_sem).wait()
    for i in range(3):
        pltpu.make_async_copy(g_ref.at[v], g_ref.at[v], x_send.at[i]).wait()
    pltpu.make_async_copy(z_ref.at[pl.ds(0, NI - 1)], z_ref.at[pl.ds(0, NI - 1)], a_send).wait()


def channelize(samples, history, fir_taps, kept_channels):
    vmem = pl.BlockSpec(memory_space=pltpu.VMEM)
    hbm = pl.BlockSpec(memory_space=pl.ANY)
    return pl.pallas_call(
        channelize_kernel,
        out_shape=jax.ShapeDtypeStruct((NY, NZ, 32, 256), jnp.bfloat16),
        in_specs=[hbm, hbm, vmem, vmem],
        out_specs=hbm,
        scratch_shapes=[
            pltpu.VMEM((FRAMES, 16, SAMPLES), jnp.bfloat16),
            pltpu.VMEM((TAPS - 1, 16, SAMPLES), jnp.bfloat16),
            pltpu.VMEM((2 * NI, SAMPLES), jnp.bfloat16),
            pltpu.VMEM((512, SAMPLES), jnp.bfloat16),
            pltpu.VMEM((512, 512), jnp.bfloat16),
            pltpu.VMEM((1024, 128), jnp.float32),
            pltpu.VMEM((NI, 8, 128), jnp.bfloat16),
            pltpu.VMEM((NV, NY, NZ, 2, 8, 128), jnp.bfloat16),
            pltpu.VMEM((NZ, NY, 32, 256), jnp.bfloat16),
            pltpu.VMEM((48, SAMPLES), jnp.bfloat16),
            pltpu.VMEM((48, 2 * NI), jnp.bfloat16),
            pltpu.VMEM((48, 2 * NI), jnp.bfloat16),
            pltpu.SemaphoreType.DMA((3,)),
            pltpu.SemaphoreType.DMA,
            pltpu.SemaphoreType.DMA,
            pltpu.SemaphoreType.REGULAR((2,)),
            pltpu.SemaphoreType.DMA,
            pltpu.SemaphoreType.DMA((8,)),
            pltpu.SemaphoreType.DMA((3,)),
            pltpu.SemaphoreType.DMA((8, 4)),
            pltpu.SemaphoreType.DMA,
        ],
        compiler_params=pltpu.CompilerParams(collective_id=0, has_side_effects=True),
    )(samples, history, fir_taps, kept_channels.reshape(1, NI))


def per_device(samples, history, fir_taps, kept_channels):
    rows = channelize(samples, history, fir_taps, kept_channels)
    return correlate(rows.reshape(NV * ROWS, 256))


def solution(mesh):
    return jax.shard_map(
        per_device,
        mesh=mesh,
        in_specs=(P("vis", "inp", None), P(None, "inp", None), P(), P()),
        out_specs=P("inp", "vis", None),
        check_vma=False,
    )
```

time: 46.5 us -> 43.7 us (0.940); the launches traced: 45.6 us -> 43.5 us
  Pallas kernels: 45.6 us -> 43.4 us
    pallas_call x2, Pallas kernels: 45.6 us -> 43.4 us  [the longest x1 39.7 us: channelize(): pl.pallas_call(channelize_kernel, out_shape=jax.ShapeDtypeStruct((NY, NZ,...]
where the time goes in v3:
time: 43.7 us; the launch traced here: 43.5 us
  Pallas kernels  43.4 us (99%)
    pallas_call x1, Pallas kernels, channelize(): pl.pallas_call(channelize_kernel, out_shape=jax.ShapeDtypeStruct((NY, NZ,...  39.7 us
    pallas_call x1, Pallas kernels, correlate(): pl.pallas_call(correlate_kernel, out_shape=jax.ShapeDtypeStruct((1, ROWS,...  3.76 us

profile of v3, /device:TPU:1, one launch (start us, length us, event | category | flops | bytes accessed | tf_op | source)
XLA Modules:
  0.0 43.5 jit_solution(10085448026444680129)
XLA Ops:
  0.0 39.7 %shard_map.46 = bf16[8,8,32,256]{3,2,1,0:T(8,128)(2,1)} custom-call(bf16[32,16,2048]{2,1,0:T(8,128)(2,1)} %samples_ref.1, bf16[3,16,2048]{2,1,0:T(8,128)(2,1)} %history_ref.1, f32[4,2048]{1,0:T(4,128)} %taps_ref.1, s32[1,128]{1,0:T(1,128)} %bitcast.3), custom_call_target="tpu_custom_call" | custom-call | tf_op jit(solution)/shard_map/pallas_call | solution.py:348
  39.7 3.8 %shard_map.47 = bf16[1,512,2048]{2,1,0:T(8,128)(2,1)} custom-call(bf16[2048,256]{1,0:T(8,128)(2,1)} %bitcast.2), custom_call_target="tpu_custom_call" | custom-call | tf_op jit(solution)/shard_map/pallas_call | solution.py:150

commit v4 on v3

--- a/solution.py
+++ b/solution.py
@@ -110,9 +110,16 @@
     z_ref[...] = wide_ref[...].reshape(NI, 8, 128).astype(jnp.bfloat16)
 
 
-def correlate_kernel(rows_ref, out_ref, im_ref, stage_ref, sem):
+def correlate_kernel(source_ref, out_ref, own, rows_ref, im_ref, stage_ref, sem, load_sem):
     v = lax.axis_index("vis")
-    own = rows_ref.at[pl.ds(pl.multiple_of(v * ROWS, ROWS), ROWS)]
+    mine = pltpu.make_async_copy(source_ref.at[pl.ds(pl.multiple_of(v * ROWS, ROWS), ROWS)], own, load_sem.at[NV])
+    mine.start()
+    loads = []
+    for j in range(NV):
+        block = pl.ds(j * ROWS, ROWS)
+        loads.append(pltpu.make_async_copy(source_ref.at[block], rows_ref.at[block], load_sem.at[j]))
+        loads[j].start()
+    mine.wait()
     real = (lax.broadcasted_iota(jnp.int32, (ROWS, 128), 1) & 32) == 0
     for pair in range(2):
         x = own[:, pair * 128 : pair * 128 + 128].astype(jnp.float32)
@@ -123,6 +130,7 @@
     scale = 1.0 / (NV * FRAMES)
     for j in range(NV):
         cols = slice(j * ROWS, j * ROWS + ROWS)
+        loads[j].wait()
 
         def product(ref, cols=cols):
             return lax.dot_general(ref[...], rows_ref[cols, :], nt, preferred_element_type=jnp.float32) * scale
@@ -150,12 +158,15 @@
     return pl.pallas_call(
         correlate_kernel,
         out_shape=jax.ShapeDtypeStruct((1, ROWS, NV * ROWS), jnp.bfloat16),
-        in_specs=[pl.BlockSpec(memory_space=pltpu.VMEM)],
+        in_specs=[pl.BlockSpec(memory_space=pl.ANY)],
         out_specs=pl.BlockSpec(memory_space=pl.ANY),
         scratch_shapes=[
             pltpu.VMEM((ROWS, 256), jnp.bfloat16),
+            pltpu.VMEM((NV * ROWS, 256), jnp.bfloat16),
+            pltpu.VMEM((ROWS, 256), jnp.bfloat16),
             pltpu.VMEM((NV, ROWS, ROWS), jnp.bfloat16),
             pltpu.SemaphoreType.DMA((NV,)),
+            pltpu.SemaphoreType.DMA((NV + 1,)),
         ],
     )(rows)
 

time: 43.7 us -> 43.5 us (level)
  no operation moved by 1% of the time
where the time goes in v4:
time: 43.5 us; the launch traced here: 43.2 us
  Pallas kernels  43.2 us (99%)
    pallas_call x1, Pallas kernels, channelize(): pl.pallas_call(channelize_kernel, out_shape=jax.ShapeDtypeStruct((NY, NZ,...  39.7 us
    pallas_call x1, Pallas kernels, correlate(): pl.pallas_call(correlate_kernel, out_shape=jax.ShapeDtypeStruct((1, ROWS,...  3.54 us

profile of v4, /device:TPU:1, one launch (start us, length us, event | category | flops | bytes accessed | tf_op | source)
XLA Modules:
  0.0 43.2 jit_solution(14195702293056356452)
XLA Ops:
  0.0 39.7 %shard_map.46 = bf16[8,8,32,256]{3,2,1,0:T(8,128)(2,1)} custom-call(bf16[32,16,2048]{2,1,0:T(8,128)(2,1)} %samples_ref.1, bf16[3,16,2048]{2,1,0:T(8,128)(2,1)} %history_ref.1, f32[4,2048]{1,0:T(4,128)} %taps_ref.1, s32[1,128]{1,0:T(1,128)} %bitcast.3), custom_call_target="tpu_custom_call" | custom-call | tf_op jit(solution)/shard_map/pallas_call | solution.py:359
  39.7 3.5 %shard_map.47 = bf16[1,512,2048]{2,1,0:T(8,128)(2,1)} custom-call(bf16[2048,256]{1,0:T(8,128)(2,1)} %bitcast.2), custom_call_target="tpu_custom_call" | custom-call | tf_op jit(solution)/shard_map/pallas_call | solution.py:158

commit v5 on v4

--- a/solution.py
+++ b/solution.py
@@ -223,7 +223,6 @@
         src_ref=tail_ref, dst_ref=head_ref, send_sem=h_send, recv_sem=h_recv, device_id=(me, right), device_id_type=MESH
     )
 
-    filter_frames(frames_ref, taps_ref, weighted_ref, 0, 4)
     pl.semaphore_wait(barrier, 2 * (NY - 1) + 6)
     tell_z()
 
@@ -231,7 +230,7 @@
     def _():
         handover.start()
 
-    filter_frames(frames_ref, taps_ref, weighted_ref, 4, 16)
+    filter_frames(frames_ref, taps_ref, weighted_ref, 0, 16)
 
     @pl.when(v > 0)
     def _():

time: 43.5 us -> 43.3 us (level)
  no operation moved by 1% of the time
where the time goes in v5:
time: 43.3 us; the launch traced here: 43 us
  Pallas kernels  43 us (99%)
    pallas_call x1, Pallas kernels, channelize(): pl.pallas_call(channelize_kernel, out_shape=jax.ShapeDtypeStruct((NY, NZ,...  39.5 us
    pallas_call x1, Pallas kernels, correlate(): pl.pallas_call(correlate_kernel, out_shape=jax.ShapeDtypeStruct((1, ROWS,...  3.54 us

profile of v5, /device:TPU:1, one launch (start us, length us, event | category | flops | bytes accessed | tf_op | source)
XLA Modules:
  0.0 43.0 jit_solution(12473594901816450325)
XLA Ops:
  0.0 39.5 %shard_map.46 = bf16[8,8,32,256]{3,2,1,0:T(8,128)(2,1)} custom-call(bf16[32,16,2048]{2,1,0:T(8,128)(2,1)} %samples_ref.1, bf16[3,16,2048]{2,1,0:T(8,128)(2,1)} %history_ref.1, f32[4,2048]{1,0:T(4,128)} %taps_ref.1, s32[1,128]{1,0:T(1,128)} %bitcast.3), custom_call_target="tpu_custom_call" | custom-call | tf_op jit(solution)/shard_map/pallas_call | solution.py:358
  39.5 3.5 %shard_map.47 = bf16[1,512,2048]{2,1,0:T(8,128)(2,1)} custom-call(bf16[2048,256]{1,0:T(8,128)(2,1)} %bitcast.2), custom_call_target="tpu_custom_call" | custom-call | tf_op jit(solution)/shard_map/pallas_call | solution.py:158
